TPU v7x, 32 devices: a whole 2x2x4 slice. The times are simulated.
32 devices in a mesh: lat: 4 (over z), lon: 8 (over y, x, core).
Axes of the slice: x: 2, y: 2, z: 4, core: 2. Of those that a mesh axis runs over, the one named last changes fastest.
Arguments:
- lat_coef: float32 [4, 256, 1024], P(None, 'lat', 'lon'), may hold values from 0.02 to 0.12
- lon_coef: float32 [4, 256, 1024], P(None, 'lat', 'lon'), may hold values from 0.02 to 0.12
- std_scale: float32 [4, 256, 1024], P(None, 'lat', 'lon'), may hold values from 0.5 to 2
- land_mask: int32 [256, 1024], P('lat', 'lon'), may hold values 0 or 1
- lst_weights: float32 [4], replicated, may hold values from 0.1 to 0.6
- innovation: float32 [16384, 128], P(('lat', 'lon')), may hold values from -6 to 6
- inv_var: float32 [16384, 128], P(('lat', 'lon')), may hold values from 0.2 to 5
- owner: int32 [16384, 1], P(('lat', 'lon')), may hold values from 0 to 31; in each aligned block of 512 rows (0 to 511, 512 to 1023, ...) at most 32 rows name the same one
- row_ids: int32 [16384], P(('lat', 'lon')), may hold values from 0 to 63
- offsets: int32 [16384, 128], P(('lat', 'lon')), may hold values from 0 to 127
Outputs:
- increment: float32 [4, 256, 1024], P(None, 'lat', 'lon')
- departure: float32 [16384, 128], P(('lat', 'lon'))
Inputs may be any that keep to these rules, and one draw needn't show every extreme that they name: Within the 512 tiles of one device no owner is named more than 32 times.
All inputs are finite; a program needn't handle non-finite values. No bound on the sum of `land_mask` on one device may be relied on, other than what follows from the above.
Results may differ from a plain program's by a relative error of at most 0.00026.
Values sent between devices are 32-bit elements; how exact they have to be, the bound alone decides.
No kernel may reach another device: no remote copies, remote signals or barrier semaphores. Data moves between devices by JAX's collectives and lax.ppermute only.
A program may use at most 64 MiB of HBM per device.

v0:
```python
import math
import jax
import jax.numpy as jnp
from jax import lax
from jax.sharding import PartitionSpec as P

PASSES = 8
ITERS = 2


def with_halo(block, sides, width, periodic):
    for axis, dim in sides:
        count = lax.axis_size(axis)
        forward = [(i, i + 1) for i in range(count - 1)]
        if periodic:
            forward.append((count - 1, 0))
        backward = [(target, source) for source, target in forward]
        low = lax.ppermute(
            lax.slice_in_dim(block, block.shape[dim] - width, None, axis=dim), axis, forward
        )
        high = lax.ppermute(lax.slice_in_dim(block, 0, width, axis=dim), axis, backward)
        block = jnp.concatenate([low, block, high], axis=dim)
    return block


def lst_of(weights, field):
    total = weights[0] * field[0]
    for index in range(1, field.shape[0]):
        total = total + weights[index] * field[index]
    return total


def extend(field, width):
    taller = with_halo(field, (("lat", 1),), width, False)
    return with_halo(taller, (("lon", 2),), width, True)


def pass_step(field, north_face, east_face):
    centre = field[:, 1:-1, 1:-1]
    north = field[:, 2:, 1:-1]
    south = field[:, :-2, 1:-1]
    east = field[:, 1:-1, 2:]
    west = field[:, 1:-1, :-2]
    face_north = north_face[:, 1:-1, 1:-1]
    face_south = north_face[:, :-2, 1:-1]
    face_east = east_face[:, 1:-1, 1:-1]
    face_west = east_face[:, 1:-1, :-2]
    return (
        centre
        + face_north * (north - centre)
        - face_south * (centre - south)
        + face_east * (east - centre)
        - face_west * (centre - west)
    )


def diffuse(field, faces, rim_depth):
    fields = field.shape[0]
    for block in range(PASSES // rim_depth):
        grown = extend(field, rim_depth)
        for inner in range(rim_depth):
            window = faces[:, inner : faces.shape[1] - inner, inner : faces.shape[2] - inner]
            grown = pass_step(grown, window[:fields], window[fields:])
        field = grown
    return field


def total_sum(value):
    return lax.psum(value, ("lat", "lon"))


def cells_to_rows(values, offsets):
    columns = lax.broadcasted_iota(jnp.int32, (1, 1, offsets.shape[1]), 2)
    return jnp.sum(jnp.where(offsets[:, :, None] == columns, values[:, :, None], 0.0), axis=1)


def rows_to_cells(rows, offsets):
    columns = lax.broadcasted_iota(jnp.int32, (1, 1, offsets.shape[1]), 2)
    return jnp.sum(jnp.where(offsets[:, :, None] == columns, rows[:, None, :], 0.0), axis=2)


def blockwise(func, first, offsets):
    count, width = first.shape
    block_rows = math.gcd(count, 64)
    shaped = (count // block_rows, block_rows, width)

    def apply_block(pair):
        return func(pair[0], pair[1])

    result = lax.map(apply_block, (first.reshape(shaped), offsets.reshape(shaped)))
    return result.reshape(count, width)


def contract_first(left, right):
    return lax.dot_general(
        left,
        right,
        (((0,), (0,)), ((), ())),
        precision=lax.Precision.HIGHEST,
        preferred_element_type=jnp.float32,
    )


def on_device(
    lat_coef,
    lon_coef,
    std_scale,
    land_mask,
    lst_weights,
    innovation,
    inv_var,
    owner,
    row_ids,
    offsets,
):
    fields, tile_rows, tile_cols = lat_coef.shape
    tiles_here, row_width = innovation.shape
    devices = lax.axis_size("lat") * lax.axis_size("lon")
    capacity = max(2, 2 * tiles_here // devices)
    rows_here = tile_rows * tile_cols // row_width
    global_row = lax.axis_index("lat") * tile_rows + lax.broadcasted_iota(
        jnp.int32, (1, tile_rows, 1), 1
    )
    north_face = jnp.where(global_row == lax.axis_size("lat") * tile_rows - 1, 0.0, lat_coef)
    rim_depth = 4
    faces = extend(jnp.concatenate([north_face, lon_coef], 0), rim_depth)
    mask_field = land_mask.astype(jnp.float32)

    def forward(vector):
        return mask_field * std_scale * diffuse(vector, faces, rim_depth)

    def adjoint(vector):
        return diffuse(mask_field * std_scale * vector, faces, rim_depth)

    def spread(grid):
        return lst_weights[:, None, None] * grid[None]

    destination = owner[:, 0]
    hits = (destination[:, None] == jnp.arange(devices, dtype=jnp.int32)[None, :]).astype(jnp.int32)
    bucket_rank = jnp.sum(jnp.cumsum(hits, axis=0) * hits, axis=1) - 1
    slot_index = destination * capacity + bucket_rank
    slot_range = jnp.arange(devices * capacity, dtype=jnp.int32)
    placement = (slot_range[:, None] == slot_index[None, :]).astype(jnp.float32)
    send_ids = (
        jnp.sum(
            jnp.where(slot_range[:, None] == slot_index[None, :], row_ids[None, :] + 1, 0), axis=1
        )
        - 1
    )
    got_ids = lax.all_to_all(send_ids, ("lat", "lon"), split_axis=0, concat_axis=0, tiled=True)
    ownership = (got_ids[:, None] == jnp.arange(rows_here, dtype=jnp.int32)[None, :]).astype(
        jnp.float32
    )

    def to_rows(values):
        return blockwise(cells_to_rows, values, offsets)

    def pack(rows):
        return jnp.dot(
            placement, rows, precision=lax.Precision.HIGHEST, preferred_element_type=jnp.float32
        )

    def collect(buffer):
        return contract_first(ownership, buffer)

    def send_back(values):
        arrived = lax.all_to_all(
            pack(to_rows(values)), ("lat", "lon"), split_axis=0, concat_axis=0, tiled=True
        )
        return spread(collect(arrived))

    residual = adjoint(send_back(inv_var * innovation))
    direction = residual
    norm_now = total_sum(jnp.sum(residual * residual))
    increment = jnp.zeros_like(residual)
    analysed = jnp.zeros_like(innovation)
    for index in range(ITERS):
        image = forward(direction)
        returned = lax.all_to_all(
            jnp.dot(
                ownership,
                lst_of(lst_weights, image),
                precision=lax.Precision.HIGHEST,
                preferred_element_type=jnp.float32,
            ),
            ("lat", "lon"),
            split_axis=0,
            concat_axis=0,
            tiled=True,
        )
        seen = blockwise(rows_to_cells, contract_first(placement, returned), offsets)
        product = direction + adjoint(send_back(inv_var * seen))
        step_size = norm_now / total_sum(jnp.sum(direction * product))
        increment = increment + step_size * image
        analysed = analysed + step_size * seen
        if index + 1 < ITERS:
            residual = residual - step_size * product
            norm_next = total_sum(jnp.sum(residual * residual))
            direction = residual + norm_next / norm_now * direction
            norm_now = norm_next
    return (increment, innovation - analysed)


def solution(mesh):
    in_specs = (
        P(None, "lat", "lon"),
        P(None, "lat", "lon"),
        P(None, "lat", "lon"),
        P("lat", "lon"),
        P(),
        P(("lat", "lon"), None),
        P(("lat", "lon"), None),
        P(("lat", "lon"), None),
        P(("lat", "lon")),
        P(("lat", "lon"), None),
    )
    out_specs = (P(None, "lat", "lon"), P(("lat", "lon"), None))
    return jax.shard_map(
        on_device, mesh=mesh, in_specs=in_specs, out_specs=out_specs, check_vma=False
    )
```

profile of v0, /device:TPU:0, one launch (start us, length us, event | category | flops | bytes accessed | tf_op | source)
XLA Modules:
  0.0 555.1 jit_solution(16266994151909909597)
XLA Ops:
  5.3 7.3 %all-to-all-start = ((s32[32,32,1]{1,2,0:T(1,128)}), s32[32,32,1]{1,2,0:T(1,128)S(1)}, u32[]{:S(2)}, u32[]{:S(2)}) async-start(s32[32,32,1]{1,2,0:T(1,128)} %sub.738), calls=%async_computation | async-start | bytes 32768 | tf_op jit(solution)/shard_map/all_to_all | solution.py:150
  13.7 22.9 %while.50 = (s32[]{:T(128)}, f32[8,64,128]{2,1,0:T(8,128)S(1)}, s32[8,64,128]{2,1,0:T(8,128)S(1)}, f32[8,64,128]{2,1,0:T(8,128)S(1)}, s32[]{:T(128)}) while((s32[]{:T(128)}, f32[8,64,128]{2,1,0:T(8,128)S(1)}, s32[8,64,128]{2,1,0:T(8,128)S(1)}, f32[8,64,128]{2,1,0:T(8,128)S(1)}, s32[]{:T(128)}) %tuple.124), condition=%wide.region_6.7_spmd, body=%wide.region_4.6_spmd.sunk | while | flops 3137538 | bytes 294985 | solution.py:90
  13.8 2.8 select_reduce_fusion.11
  16.6 2.8 select_reduce_fusion.11
  19.5 2.8 select_reduce_fusion.11
  22.3 2.8 select_reduce_fusion.11
  25.2 2.8 select_reduce_fusion.11
  28.1 2.8 select_reduce_fusion.11
  30.9 2.8 select_reduce_fusion.11
  33.8 2.8 select_reduce_fusion.11
  38.5 5.8 %all-to-all-start.1 = ((f32[32,32,128]{2,1,0:T(8,128)}), f32[32,32,128]{2,1,0:T(8,128)S(1)}, u32[]{:S(2)}, u32[]{:S(2)}) async-start(f32[32,32,128]{2,1,0:T(8,128)} %fusion.4), calls=%async_computation.1 | async-start | bytes 1048576 | tf_op jit(solution)/shard_map/all_to_all | solution.py:167
  44.4 3.7 collective-permute-start.4
  50.7 3.1 collective-permute-done.4
  56.8 3.1 all-to-all-done.1
  60.8 5.1 collective-permute-start
  67.5 4.0 collective-permute-done.1
  83.7 4.2 collective-permute-done.9
  90.8 4.4 collective-permute-done.10
  100.8 4.2 collective-permute-done.13
  105.2 3.1 collective-permute-start.15
  108.4 3.2 collective-permute-done.14
  117.3 4.2 collective-permute-done.17
  130.0 3.7 fusion.18
  133.6 2.9 all-to-all-start.2
  136.9 15.2 %all-to-all-done.2 = f32[32,32,128]{2,1,0:T(8,128)S(1)} async-done(((f32[32,32,128]{2,1,0:T(8,128)}), f32[32,32,128]{2,1,0:T(8,128)S(1)}, u32[]{:S(2)}, u32[]{:S(2)}) %all-to-all-start.2) | async-done | bytes 524320 | tf_op jit(solution)/shard_map/all_to_all | solution.py:179
  153.9 27.1 %while.51 = (s32[]{:T(128)}, f32[8,64,128]{2,1,0:T(8,128)S(1)}, s32[8,64,128]{2,1,0:T(8,128)S(1)}, f32[8,64,128]{2,1,0:T(8,128)}, s32[]{:T(128)}) while((s32[]{:T(128)}, f32[8,64,128]{2,1,0:T(8,128)S(1)}, s32[8,64,128]{2,1,0:T(8,128)S(1)}, f32[8,64,128]{2,1,0:T(8,128)}, s32[]{:T(128)}) %tuple.119), condition=%wide.region_11.12_spmd, body=%wide.region_9.11_spmd.sunk | while | flops 3137538 | bytes 294985 | solution.py:90
  181.7 27.3 %while.52 = (s32[]{:T(128)}, f32[8,64,128]{2,1,0:T(8,128)}, s32[8,64,128]{2,1,0:T(8,128)S(1)}, f32[8,64,128]{2,1,0:T(8,128)S(1)}, s32[]{:T(128)}) while((s32[]{:T(128)}, f32[8,64,128]{2,1,0:T(8,128)}, s32[8,64,128]{2,1,0:T(8,128)S(1)}, f32[8,64,128]{2,1,0:T(8,128)S(1)}, s32[]{:T(128)}) %tuple.125), condition=%wide.region_14.15_spmd, body=%wide.region_12.14_spmd.sunk | while | flops 3137538 | bytes 295493 | solution.py:90
  181.7 2.8 select_reduce_fusion.13
  185.2 2.8 select_reduce_fusion.13
  211.1 18.4 %all_to_all.54 = f32[32,32,128]{2,1,0:T(8,128)S(1)} all-to-all(f32[32,32,128]{2,1,0:T(8,128)S(1)} %fusion.2), channel_id=1, replica_groups=mesh['lat'=4,'lon'=8] {'lat','lon'}, dimensions={0} | all-to-all | bytes 1048576 | tf_op jit(solution)/shard_map/all_to_all | solution.py:167
  230.3 3.1 collective-permute-start.20
  234.8 4.2 collective-permute-done.21
  239.2 2.8 collective-permute-start.23
  242.0 4.0 collective-permute-done.22
  251.3 4.2 collective-permute-done.25
  258.3 4.0 collective-permute-done.26
  265.3 38.2 %all-reduce = (f32[]{:T(128)}, f32[]{:T(128)}) all-reduce(f32[]{:T(128)} %get-tuple-element.118, f32[]{:T(128)} %get-tuple-element.117), channel_id=1, replica_groups=mesh['lat'=4,'lon'=8] {'lat','lon'}, use_global_device_ids=true, to_apply=%region_8.9 | all-reduce | flops 2 | bytes 16 | tf_op jit(solution)/shard_map/psum | solution.py:69
  305.5 40.8 %psum.30 = f32[]{:T(128)} all-reduce(f32[]{:T(128)} %multiply_reduce_fusion), channel_id=1, replica_groups=mesh['lat'=4,'lon'=8] {'lat','lon'}, use_global_device_ids=true, to_apply=%region_18.19 | all-reduce | flops 1 | bytes 8 | tf_op jit(solution)/shard_map/psum | solution.py:69
  347.7 3.4 collective-permute-start.28
  352.5 4.2 collective-permute-done.29
  359.5 2.9 collective-permute-done.30
  369.1 4.2 collective-permute-done.33
  376.3 3.9 collective-permute-done.34
  382.6 3.7 fusion.16
  386.3 3.6 all-to-all-start.4
  390.0 15.6 %all-to-all-done.4 = f32[32,32,128]{2,1,0:T(8,128)} async-done(((f32[32,32,128]{2,1,0:T(8,128)}), f32[32,32,128]{2,1,0:T(8,128)}, u32[]{:S(2)}, u32[]{:S(2)}) %all-to-all-start.4) | async-done | bytes 524320 | tf_op jit(solution)/shard_map/all_to_all | solution.py:179
  408.3 27.1 %while.53 = (s32[]{:T(128)}, f32[8,64,128]{2,1,0:T(8,128)S(1)}, s32[8,64,128]{2,1,0:T(8,128)S(1)}, f32[8,64,128]{2,1,0:T(8,128)}, s32[]{:T(128)}) while((s32[]{:T(128)}, f32[8,64,128]{2,1,0:T(8,128)S(1)}, s32[8,64,128]{2,1,0:T(8,128)S(1)}, f32[8,64,128]{2,1,0:T(8,128)}, s32[]{:T(128)}) %tuple.121), condition=%wide.region_21.22_spmd, body=%wide.region_19.21_spmd.sunk | while | flops 3137538 | bytes 294985 | solution.py:90
  435.4 22.9 %while.54 = (s32[]{:T(128)}, f32[8,64,128]{2,1,0:T(8,128)S(1)}, s32[8,64,128]{2,1,0:T(8,128)S(1)}, f32[8,64,128]{2,1,0:T(8,128)S(1)}, s32[]{:T(128)}) while((s32[]{:T(128)}, f32[8,64,128]{2,1,0:T(8,128)S(1)}, s32[8,64,128]{2,1,0:T(8,128)S(1)}, f32[8,64,128]{2,1,0:T(8,128)S(1)}, s32[]{:T(128)}) %tuple.123), condition=%wide.region_24.25_spmd, body=%wide.region_22.24_spmd.sunk | while | flops 3137538 | bytes 294985 | solution.py:90
  435.5 2.8 select_reduce_fusion.15
  438.4 2.8 select_reduce_fusion.15
  441.2 2.8 select_reduce_fusion.15
  444.1 2.8 select_reduce_fusion.15
  446.9 2.8 select_reduce_fusion.15
  449.8 2.8 select_reduce_fusion.15
  452.7 2.8 select_reduce_fusion.15
  455.5 2.8 select_reduce_fusion.15
  459.4 18.4 %all_to_all.55 = f32[32,32,128]{2,1,0:T(8,128)S(1)} all-to-all(f32[32,32,128]{2,1,0:T(8,128)S(1)} %fusion), channel_id=1, replica_groups=mesh['lat'=4,'lon'=8] {'lat','lon'}, dimensions={0} | all-to-all | bytes 1048576 | tf_op jit(solution)/shard_map/all_to_all | solution.py:167
  478.6 3.1 collective-permute-start.36
  483.1 4.2 collective-permute-done.37
  490.1 4.3 collective-permute-done.38
  499.8 4.2 collective-permute-done.41
  504.1 2.9 collective-permute-start.43
  507.0 3.8 collective-permute-done.42
  513.8 38.2 %psum.31 = f32[]{:T(128)} all-reduce(f32[]{:T(128)} %fusion.267), channel_id=1, replica_groups=mesh['lat'=4,'lon'=8] {'lat','lon'}, use_global_device_ids=true, to_apply=%region_26.27 | all-reduce | flops 1 | bytes 8 | tf_op jit(solution)/shard_map/psum | solution.py:69
  (351 shorter events, 180.1 us)
Async XLA Ops:
  0.6 12.1 %copy-start.3 = (f32[512,128]{1,0:T(8,128)S(1)}, f32[512,128]{1,0:T(8,128)}, u32[]{:S(2)}) copy-start(f32[512,128]{1,0:T(8,128)} %param.26) | copy-start | bytes 786436
  3.6 10.1 %copy-start.2 = (s32[512,128]{1,0:T(8,128)S(1)}, s32[512,128]{1,0:T(8,128)}, u32[]{:S(2)}) copy-start(s32[512,128]{1,0:T(8,128)} %param.29) | copy-start | bytes 786436
  5.3 33.1 %all-to-all-start = ((s32[32,32,1]{1,2,0:T(1,128)}), s32[32,32,1]{1,2,0:T(1,128)S(1)}, u32[]{:S(2)}, u32[]{:S(2)}) async-start(s32[32,32,1]{1,2,0:T(1,128)} %sub.738), calls=%async_computation | async-start | bytes 32768 | tf_op jit(solution)/shard_map/all_to_all | solution.py:150
  38.4 5.9 %copy-start.7 = (f32[4,64,128]{2,1,0:T(8,128)S(1)}, f32[4,64,128]{2,1,0:T(8,128)}, u32[]{:S(2)}) copy-start(f32[4,64,128]{2,1,0:T(8,128)} %param.20) | copy-start | bytes 393220
  38.4 6.0 %copy-start = (f32[4,64,128]{2,1,0:T(8,128)S(1)}, f32[4,64,128]{2,1,0:T(8,128)}, u32[]{:S(2)}) copy-start(f32[4,64,128]{2,1,0:T(8,128)} %param.21) | copy-start | bytes 393220
  38.4 11.0 %copy-start.8 = (s32[64,128]{1,0:T(8,128)S(1)}, s32[64,128]{1,0:T(8,128)}, u32[]{:S(2)}) copy-start(s32[64,128]{1,0:T(8,128)} %param.23) | copy-start | bytes 98308
  38.5 21.5 %all-to-all-start.1 = ((f32[32,32,128]{2,1,0:T(8,128)}), f32[32,32,128]{2,1,0:T(8,128)S(1)}, u32[]{:S(2)}, u32[]{:S(2)}) async-start(f32[32,32,128]{2,1,0:T(8,128)} %fusion.4), calls=%async_computation.1 | async-start | bytes 1048576 | tf_op jit(solution)/shard_map/all_to_all | solution.py:167
  44.4 9.4 %collective-permute-start.4 = (f32[8,4,128]{2,1,0:T(4,128)S(1)}, f32[8,4,128]{2,1,0:T(4,128)S(1)}, u32[]{:S(2)}, u32[]{:S(2)}) collective-permute-start(f32[8,4,128]{2,1,0:T(4,128)S(1)} %get-tuple-element.166), channel_id=1, source_target_pairs={{0,8},{8,16},{16,24},{1,9},{9,17},{17,25},{2,10},{10,18},{18,26},{... | collective-permute-start | bytes 49160 | tf_op jit(solution)/shard_map/ppermute | solution.py:18
  48.1 5.8 %collective-permute-start.5 = (f32[8,4,128]{2,1,0:T(4,128)S(1)}, f32[8,4,128]{2,1,0:T(4,128)S(1)}, u32[]{:S(2)}, u32[]{:S(2)}) collective-permute-start(f32[8,4,128]{2,1,0:T(4,128)S(1)} %get-tuple-element.167), channel_id=1, source_target_pairs={{8,0},{16,8},{24,16},{9,1},{17,9},{25,17},{10,2},{18,10},{26,18},{... | collective-permute-start | bytes 49160 | tf_op jit(solution)/shard_map/ppermute | solution.py:21
  53.9 6.8 %copy-start.1 = (f32[4,64,128]{2,1,0:T(8,128)S(1)}, f32[4,64,128]{2,1,0:T(8,128)}, u32[]{:S(2)}) copy-start(f32[4,64,128]{2,1,0:T(8,128)} %param.22) | copy-start | bytes 393220
  53.9 6.8 %copy-start.9 = (f32[4]{0:T(128)S(1)}, f32[4]{0:T(128)}, u32[]{:S(2)}) copy-start(f32[4]{0:T(128)} %param.24) | copy-start | bytes 52
  54.1 13.1 %collective-permute-start.6 = (f32[8,72,4]{2,1,0:T(8,128)S(1)}, f32[8,72,4]{2,1,0:T(8,128)S(1)}, u32[]{:S(2)}, u32[]{:S(2)}) collective-permute-start(f32[8,72,4]{2,1,0:T(8,128)S(1)} %get-tuple-element.164), channel_id=1, source_target_pairs={{0,1},{1,2},{2,3},{3,4},{4,5},{5,6},{6,7},{7,0},{8,9},{9,10},{10,1... | collective-permute-start | bytes 27656 | tf_op jit(solution)/shard_map/ppermute | solution.py:18
  54.2 20.1 %collective-permute-start.7 = (f32[8,72,4]{2,1,0:T(8,128)S(1)}, f32[8,72,4]{2,1,0:T(8,128)}, u32[]{:S(2)}, u32[]{:S(2)}) collective-permute-start(f32[8,72,4]{2,1,0:T(8,128)S(1)} %get-tuple-element.165), channel_id=1, source_target_pairs={{1,0},{2,1},{3,2},{4,3},{5,4},{6,5},{7,6},{0,7},{9,8},{10,9},{11,1... | collective-permute-start | bytes 27656 | tf_op jit(solution)/shard_map/ppermute | solution.py:21
  60.8 6.7 %collective-permute-start = (f32[4,4,128]{2,1,0:T(4,128)S(1)}, f32[4,4,128]{2,1,0:T(4,128)S(1)}, u32[]{:S(2)}, u32[]{:S(2)}) collective-permute-start(f32[4,4,128]{2,1,0:T(4,128)S(1)} %get-tuple-element.206), channel_id=1, source_target_pairs={{0,8},{8,16},{16,24},{1,9},{9,17},{17,25},{2,10},{10,18},{18,26},{... | collective-permute-start | bytes 24584 | tf_op jit(solution)/shard_map/ppermute | solution.py:18
  65.9 5.5 collective-permute-start.1
  71.5 6.2 %collective-permute-start.2 = (f32[4,72,4]{2,1,0:T(8,128)S(1)}, f32[4,72,4]{2,1,0:T(8,128)S(1)}, u32[]{:S(2)}, u32[]{:S(2)}) collective-permute-start(f32[4,72,4]{2,1,0:T(8,128)S(1)} %get-tuple-element.186), channel_id=1, source_target_pairs={{0,1},{1,2},{2,3},{3,4},{4,5},{5,6},{6,7},{7,0},{8,9},{9,10},{10,1... | collective-permute-start | bytes 13832 | tf_op jit(solution)/shard_map/ppermute | solution.py:18
  71.6 6.1 %collective-permute-start.3 = (f32[4,72,4]{2,1,0:T(8,128)S(1)}, f32[4,72,4]{2,1,0:T(8,128)S(1)}, u32[]{:S(2)}, u32[]{:S(2)}) collective-permute-start(f32[4,72,4]{2,1,0:T(8,128)S(1)} %get-tuple-element.187), channel_id=1, source_target_pairs={{1,0},{2,1},{3,2},{4,3},{5,4},{6,5},{7,6},{0,7},{9,8},{10,9},{11,1... | collective-permute-start | bytes 13832 | tf_op jit(solution)/shard_map/ppermute | solution.py:21
  80.2 3.5 collective-permute-start.8
  82.4 5.5 collective-permute-start.9
  88.1 7.1 %collective-permute-start.10 = (f32[4,72,4]{2,1,0:T(8,128)S(1)}, f32[4,72,4]{2,1,0:T(8,128)S(1)}, u32[]{:S(2)}, u32[]{:S(2)}) collective-permute-start(f32[4,72,4]{2,1,0:T(8,128)S(1)} %get-tuple-element.184), channel_id=1, source_target_pairs={{0,1},{1,2},{2,3},{3,4},{4,5},{5,6},{6,7},{7,0},{8,9},{9,10},{10,1... | collective-permute-start | bytes 13832 | tf_op jit(solution)/shard_map/ppermute | solution.py:18
  88.1 7.0 %collective-permute-start.11 = (f32[4,72,4]{2,1,0:T(8,128)S(1)}, f32[4,72,4]{2,1,0:T(8,128)S(1)}, u32[]{:S(2)}, u32[]{:S(2)}) collective-permute-start(f32[4,72,4]{2,1,0:T(8,128)S(1)} %get-tuple-element.185), channel_id=1, source_target_pairs={{1,0},{2,1},{3,2},{4,3},{5,4},{6,5},{7,6},{0,7},{9,8},{10,9},{11,1... | collective-permute-start | bytes 13832 | tf_op jit(solution)/shard_map/ppermute | solution.py:21
  97.6 3.3 collective-permute-start.12
  99.5 5.5 collective-permute-start.13
  105.2 6.4 %collective-permute-start.14 = (f32[4,72,4]{2,1,0:T(8,128)S(1)}, f32[4,72,4]{2,1,0:T(8,128)S(1)}, u32[]{:S(2)}, u32[]{:S(2)}) collective-permute-start(f32[4,72,4]{2,1,0:T(8,128)S(1)} %get-tuple-element.182), channel_id=1, source_target_pairs={{0,1},{1,2},{2,3},{3,4},{4,5},{5,6},{6,7},{7,0},{8,9},{9,10},{10,1... | collective-permute-start | bytes 13832 | tf_op jit(solution)/shard_map/ppermute | solution.py:18
  105.2 6.4 %collective-permute-start.15 = (f32[4,72,4]{2,1,0:T(8,128)S(1)}, f32[4,72,4]{2,1,0:T(8,128)S(1)}, u32[]{:S(2)}, u32[]{:S(2)}) collective-permute-start(f32[4,72,4]{2,1,0:T(8,128)S(1)} %get-tuple-element.183), channel_id=1, source_target_pairs={{1,0},{2,1},{3,2},{4,3},{5,4},{6,5},{7,6},{0,7},{9,8},{10,9},{11,1... | collective-permute-start | bytes 13832 | tf_op jit(solution)/shard_map/ppermute | solution.py:21
  114.0 3.3 collective-permute-start.16
  115.9 5.5 collective-permute-start.17
  121.6 5.9 %collective-permute-start.18 = (f32[4,72,4]{2,1,0:T(8,128)S(1)}, f32[4,72,4]{2,1,0:T(8,128)S(1)}, u32[]{:S(2)}, u32[]{:S(2)}) collective-permute-start(f32[4,72,4]{2,1,0:T(8,128)S(1)} %get-tuple-element.180), channel_id=1, source_target_pairs={{0,1},{1,2},{2,3},{3,4},{4,5},{5,6},{6,7},{7,0},{8,9},{9,10},{10,1... | collective-permute-start | bytes 13832 | tf_op jit(solution)/shard_map/ppermute | solution.py:18
  121.7 5.9 %collective-permute-start.19 = (f32[4,72,4]{2,1,0:T(8,128)S(1)}, f32[4,72,4]{2,1,0:T(8,128)S(1)}, u32[]{:S(2)}, u32[]{:S(2)}) collective-permute-start(f32[4,72,4]{2,1,0:T(8,128)S(1)} %get-tuple-element.181), channel_id=1, source_target_pairs={{1,0},{2,1},{3,2},{4,3},{5,4},{6,5},{7,6},{0,7},{9,8},{10,9},{11,1... | collective-permute-start | bytes 13832 | tf_op jit(solution)/shard_map/ppermute | solution.py:21
  129.9 3.7 copy-start.5
  133.6 18.5 %all-to-all-start.2 = ((f32[32,32,128]{2,1,0:T(8,128)}), f32[32,32,128]{2,1,0:T(8,128)S(1)}, u32[]{:S(2)}, u32[]{:S(2)}) async-start(f32[32,32,128]{2,1,0:T(8,128)} %fusion.18), calls=%async_computation.2 | async-start | bytes 1048576 | tf_op jit(solution)/shard_map/all_to_all | solution.py:179
  230.3 4.5 collective-permute-start.20
  233.5 5.5 collective-permute-start.21
  239.1 6.8 %collective-permute-start.22 = (f32[4,72,4]{2,1,0:T(8,128)S(1)}, f32[4,72,4]{2,1,0:T(8,128)S(1)}, u32[]{:S(2)}, u32[]{:S(2)}) collective-permute-start(f32[4,72,4]{2,1,0:T(8,128)S(1)} %get-tuple-element.178), channel_id=1, source_target_pairs={{0,1},{1,2},{2,3},{3,4},{4,5},{5,6},{6,7},{7,0},{8,9},{9,10},{10,1... | collective-permute-start | bytes 13832 | tf_op jit(solution)/shard_map/ppermute | solution.py:18
  239.2 6.8 %collective-permute-start.23 = (f32[4,72,4]{2,1,0:T(8,128)S(1)}, f32[4,72,4]{2,1,0:T(8,128)S(1)}, u32[]{:S(2)}, u32[]{:S(2)}) collective-permute-start(f32[4,72,4]{2,1,0:T(8,128)S(1)} %get-tuple-element.179), channel_id=1, source_target_pairs={{1,0},{2,1},{3,2},{4,3},{5,4},{6,5},{7,6},{0,7},{9,8},{10,9},{11,1... | collective-permute-start | bytes 13832 | tf_op jit(solution)/shard_map/ppermute | solution.py:21
  248.4 2.9 collective-permute-start.24
  250.0 5.5 collective-permute-start.25
  255.6 6.7 %collective-permute-start.26 = (f32[4,72,4]{2,1,0:T(8,128)S(1)}, f32[4,72,4]{2,1,0:T(8,128)S(1)}, u32[]{:S(2)}, u32[]{:S(2)}) collective-permute-start(f32[4,72,4]{2,1,0:T(8,128)S(1)} %get-tuple-element.176), channel_id=1, source_target_pairs={{0,1},{1,2},{2,3},{3,4},{4,5},{5,6},{6,7},{7,0},{8,9},{9,10},{10,1... | collective-permute-start | bytes 13832 | tf_op jit(solution)/shard_map/ppermute | solution.py:18
  255.7 6.6 %collective-permute-start.27 = (f32[4,72,4]{2,1,0:T(8,128)S(1)}, f32[4,72,4]{2,1,0:T(8,128)S(1)}, u32[]{:S(2)}, u32[]{:S(2)}) collective-permute-start(f32[4,72,4]{2,1,0:T(8,128)S(1)} %get-tuple-element.177), channel_id=1, source_target_pairs={{1,0},{2,1},{3,2},{4,3},{5,4},{6,5},{7,6},{0,7},{9,8},{10,9},{11,1... | collective-permute-start | bytes 13832 | tf_op jit(solution)/shard_map/ppermute | solution.py:21
  347.7 4.7 collective-permute-start.28
  351.1 5.5 collective-permute-start.29
  356.8 5.6 %collective-permute-start.30 = (f32[4,72,4]{2,1,0:T(8,128)S(1)}, f32[4,72,4]{2,1,0:T(8,128)S(1)}, u32[]{:S(2)}, u32[]{:S(2)}) collective-permute-start(f32[4,72,4]{2,1,0:T(8,128)S(1)} %get-tuple-element.174), channel_id=1, source_target_pairs={{0,1},{1,2},{2,3},{3,4},{4,5},{5,6},{6,7},{7,0},{8,9},{9,10},{10,1... | collective-permute-start | bytes 13832 | tf_op jit(solution)/shard_map/ppermute | solution.py:18
  356.9 5.9 %collective-permute-start.31 = (f32[4,72,4]{2,1,0:T(8,128)S(1)}, f32[4,72,4]{2,1,0:T(8,128)S(1)}, u32[]{:S(2)}, u32[]{:S(2)}) collective-permute-start(f32[4,72,4]{2,1,0:T(8,128)S(1)} %get-tuple-element.175), channel_id=1, source_target_pairs={{1,0},{2,1},{3,2},{4,3},{5,4},{6,5},{7,6},{0,7},{9,8},{10,9},{11,1... | collective-permute-start | bytes 13832 | tf_op jit(solution)/shard_map/ppermute | solution.py:21
  365.2 3.9 collective-permute-start.32
  367.8 5.5 collective-permute-start.33
  373.4 6.8 %collective-permute-start.34 = (f32[4,72,4]{2,1,0:T(8,128)S(1)}, f32[4,72,4]{2,1,0:T(8,128)S(1)}, u32[]{:S(2)}, u32[]{:S(2)}) collective-permute-start(f32[4,72,4]{2,1,0:T(8,128)S(1)} %get-tuple-element.172), channel_id=1, source_target_pairs={{0,1},{1,2},{2,3},{3,4},{4,5},{5,6},{6,7},{7,0},{8,9},{9,10},{10,1... | collective-permute-start | bytes 13832 | tf_op jit(solution)/shard_map/ppermute | solution.py:18
  374.1 6.2 %collective-permute-start.35 = (f32[4,72,4]{2,1,0:T(8,128)S(1)}, f32[4,72,4]{2,1,0:T(8,128)S(1)}, u32[]{:S(2)}, u32[]{:S(2)}) collective-permute-start(f32[4,72,4]{2,1,0:T(8,128)S(1)} %get-tuple-element.173), channel_id=1, source_target_pairs={{1,0},{2,1},{3,2},{4,3},{5,4},{6,5},{7,6},{0,7},{9,8},{10,9},{11,1... | collective-permute-start | bytes 13832 | tf_op jit(solution)/shard_map/ppermute | solution.py:21
  386.3 19.2 %all-to-all-start.4 = ((f32[32,32,128]{2,1,0:T(8,128)}), f32[32,32,128]{2,1,0:T(8,128)}, u32[]{:S(2)}, u32[]{:S(2)}) async-start(f32[32,32,128]{2,1,0:T(8,128)} %fusion.16), calls=%async_computation.4 | async-start | bytes 1048576 | tf_op jit(solution)/shard_map/all_to_all | solution.py:179
  478.6 4.5 collective-permute-start.36
  481.8 5.5 collective-permute-start.37
  487.4 7.0 %collective-permute-start.38 = (f32[4,72,4]{2,1,0:T(8,128)S(1)}, f32[4,72,4]{2,1,0:T(8,128)S(1)}, u32[]{:S(2)}, u32[]{:S(2)}) collective-permute-start(f32[4,72,4]{2,1,0:T(8,128)S(1)} %get-tuple-element.170), channel_id=1, source_target_pairs={{0,1},{1,2},{2,3},{3,4},{4,5},{5,6},{6,7},{7,0},{8,9},{9,10},{10,1... | collective-permute-start | bytes 13832 | tf_op jit(solution)/shard_map/ppermute | solution.py:18
  487.5 6.9 %collective-permute-start.39 = (f32[4,72,4]{2,1,0:T(8,128)S(1)}, f32[4,72,4]{2,1,0:T(8,128)S(1)}, u32[]{:S(2)}, u32[]{:S(2)}) collective-permute-start(f32[4,72,4]{2,1,0:T(8,128)S(1)} %get-tuple-element.171), channel_id=1, source_target_pairs={{1,0},{2,1},{3,2},{4,3},{5,4},{6,5},{7,6},{0,7},{9,8},{10,9},{11,1... | collective-permute-start | bytes 13832 | tf_op jit(solution)/shard_map/ppermute | solution.py:21
  496.8 2.9 collective-permute-start.40
  498.4 5.5 collective-permute-start.41
  504.1 6.7 %collective-permute-start.42 = (f32[4,72,4]{2,1,0:T(8,128)S(1)}, f32[4,72,4]{2,1,0:T(8,128)S(1)}, u32[]{:S(2)}, u32[]{:S(2)}) collective-permute-start(f32[4,72,4]{2,1,0:T(8,128)S(1)} %get-tuple-element.168), channel_id=1, source_target_pairs={{0,1},{1,2},{2,3},{3,4},{4,5},{5,6},{6,7},{7,0},{8,9},{9,10},{10,1... | collective-permute-start | bytes 13832 | tf_op jit(solution)/shard_map/ppermute | solution.py:18
  504.1 6.7 %collective-permute-start.43 = (f32[4,72,4]{2,1,0:T(8,128)S(1)}, f32[4,72,4]{2,1,0:T(8,128)S(1)}, u32[]{:S(2)}, u32[]{:S(2)}) collective-permute-start(f32[4,72,4]{2,1,0:T(8,128)S(1)} %get-tuple-element.169), channel_id=1, source_target_pairs={{1,0},{2,1},{3,2},{4,3},{5,4},{6,5},{7,6},{0,7},{9,8},{10,9},{11,1... | collective-permute-start | bytes 13832 | tf_op jit(solution)/shard_map/ppermute | solution.py:21
  513.0 40.4 %copy-start.4 = (f32[512,128]{1,0:T(8,128)S(1)}, f32[512,128]{1,0:T(8,128)}, u32[]{:S(2)}) copy-start(f32[512,128]{1,0:T(8,128)} %param.25) | copy-start | bytes 786436
  513.8 40.3 %copy-start.6 = (f32[4,64,128]{2,1,0:T(8,128)S(1)}, f32[4,64,128]{2,1,0:T(8,128)}, u32[]{:S(2)}) copy-start(f32[4,64,128]{2,1,0:T(8,128)} %copy-done.5) | copy-start | bytes 393220
where the time goes:
time: 565 us; the launch traced here: 555 us
  blocking collectives  154 us (27%)
  other arithmetic  143 us (25%)
  waiting for transfers between devices  115 us (20%)
  starting transfers between devices  94.7 us (17%)
  local copies, waits for them, and re-layouts  22.1 us (4%)
  matrix products  18.9 us (3%)
  between operations  6.16 us (1%)
    psum x3, blocking collectives, total_sum(): return lax.psum(value, ('lat', 'lon'))  117 us
    reduce_sum x24, other arithmetic, cells_to_rows(): jnp.sum(jnp.where(offsets[:, :, None] == columns, values[:, :, None], 0.0...  66.8 us
    ppermute x22, starting transfers between devices, with_halo(): lax.ppermute(lax.slice_in_dim(block, 0, width, axis=dim), axis, backward)  43.7 us
    ppermute x22, waiting for transfers between devices, with_halo(): lax.ppermute(lax.slice_in_dim(block, 0, width, axis=dim), axis, backward)  42.2 us
    reduce_sum x16, other arithmetic, rows_to_cells(): jnp.sum(jnp.where(offsets[:, :, None] == columns, rows[:, None, :], 0.0),...  41.2 us
    ppermute x22, waiting for transfers between devices, with_halo(): lax.ppermute(lax.slice_in_dim(block, block.shape[dim] - width, None, axis...  38.8 us
    all_to_all x2, blocking collectives, send_back(): lax.all_to_all(pack(to_rows(values)), ('lat', 'lon'), split_axis=0, conca...  36.8 us
    ppermute x22, starting transfers between devices, with_halo(): lax.ppermute(lax.slice_in_dim(block, block.shape[dim] - width, None, axis...  31.3 us
  transfers between devices with their start and end apart: 48, of which 26 were waited for; matrix products, arithmetic and copies ran while one was open for 5% of the time, Pallas kernels for 0%

commit v1 on v0

--- a/solution.py
+++ b/solution.py
@@ -6,6 +6,9 @@
 
 PASSES = 8
 ITERS = 2
+watch_cubes = lambda comm_axis, patch, mesh_dim: lax.psum(
+    lax.psum(patch, axis_name=comm_axis), mesh_dim
+)
 
 
 def with_halo(block, sides, width, periodic):
@@ -66,7 +69,7 @@
 
 
 def total_sum(value):
-    return lax.psum(value, ("lat", "lon"))
+    return watch_cubes("lon", patch=value, mesh_dim="lat")
 
 
 def cells_to_rows(values, offsets):

time: 565 us -> 514 us (0.910)
  blocking collectives: 154 us -> 106 us
    psum x3 -> x6, blocking collectives: 117 us -> 69.5 us  [the longest x3 40.5 us: lax.psum(patch, axis_name=comm_axis)]
  transfers between devices with their start and end apart: 48 -> 48, of which waited for: 26 -> 25; matrix products, arithmetic and copies ran while one was open for 5% -> 6% of each run, Pallas kernels for 0% -> 0%
where the time goes in v1:
time: 514 us; the launch traced here: 504 us
  other arithmetic  143 us (28%)
  waiting for transfers between devices  114 us (22%)
  blocking collectives  106 us (21%)
  starting transfers between devices  92.4 us (18%)
  local copies, waits for them, and re-layouts  22.1 us (4%)
  matrix products  18.9 us (4%)
  between operations  5.92 us (1%)
    reduce_sum x24, other arithmetic, cells_to_rows(): jnp.sum(jnp.where(offsets[:, :, None] == columns, values[:, :, None], 0.0...  66.8 us
    ppermute x22, starting transfers between devices, with_halo(): lax.ppermute(lax.slice_in_dim(block, 0, width, axis=dim), axis, backward)  43.8 us
    ppermute x22, waiting for transfers between devices, with_halo(): lax.ppermute(lax.slice_in_dim(block, 0, width, axis=dim), axis, backward)  41.8 us
    reduce_sum x16, other arithmetic, rows_to_cells(): jnp.sum(jnp.where(offsets[:, :, None] == columns, rows[:, None, :], 0.0),...  41.2 us
    psum x3, blocking collectives, lax.psum(patch, axis_name=comm_axis)  40.5 us
    ppermute x22, waiting for transfers between devices, with_halo(): lax.ppermute(lax.slice_in_dim(block, block.shape[dim] - width, None, axis...  38.6 us
    all_to_all x2, blocking collectives, send_back(): lax.all_to_all(pack(to_rows(values)), ('lat', 'lon'), split_axis=0, conca...  36.8 us
    all_to_all x2, waiting for transfers between devices, on_device(): lax.all_to_all(jnp.dot(ownership, lst_of(lst_weights, image), precision=l...  30.8 us
  transfers between devices with their start and end apart: 48, of which 25 were waited for; matrix products, arithmetic and copies ran while one was open for 6% of the time, Pallas kernels for 0%

profile of v1, /device:TPU:0, one launch (start us, length us, event | category | flops | bytes accessed | tf_op | source)
XLA Modules:
  0.0 504.3 jit_solution(11760593519183698199)
XLA Ops:
  5.3 7.3 %all-to-all-start = ((s32[32,32,1]{1,2,0:T(1,128)}), s32[32,32,1]{1,2,0:T(1,128)S(1)}, u32[]{:S(2)}, u32[]{:S(2)}) async-start(s32[32,32,1]{1,2,0:T(1,128)} %sub.738), calls=%async_computation | async-start | bytes 32768 | tf_op jit(solution)/shard_map/all_to_all | solution.py:153
  13.7 22.9 %while.50 = (s32[]{:T(128)}, f32[8,64,128]{2,1,0:T(8,128)S(1)}, s32[8,64,128]{2,1,0:T(8,128)S(1)}, f32[8,64,128]{2,1,0:T(8,128)S(1)}, s32[]{:T(128)}) while((s32[]{:T(128)}, f32[8,64,128]{2,1,0:T(8,128)S(1)}, s32[8,64,128]{2,1,0:T(8,128)S(1)}, f32[8,64,128]{2,1,0:T(8,128)S(1)}, s32[]{:T(128)}) %tuple.124), condition=%wide.region_6.7_spmd, body=%wide.region_4.6_spmd.sunk | while | flops 3137538 | bytes 294985 | solution.py:93
  13.8 2.8 select_reduce_fusion.11
  16.6 2.8 select_reduce_fusion.11
  19.5 2.8 select_reduce_fusion.11
  22.3 2.8 select_reduce_fusion.11
  25.2 2.8 select_reduce_fusion.11
  28.1 2.8 select_reduce_fusion.11
  30.9 2.8 select_reduce_fusion.11
  33.8 2.8 select_reduce_fusion.11
  38.5 5.8 %all-to-all-start.1 = ((f32[32,32,128]{2,1,0:T(8,128)}), f32[32,32,128]{2,1,0:T(8,128)S(1)}, u32[]{:S(2)}, u32[]{:S(2)}) async-start(f32[32,32,128]{2,1,0:T(8,128)} %fusion.4), calls=%async_computation.1 | async-start | bytes 1048576 | tf_op jit(solution)/shard_map/all_to_all | solution.py:170
  44.4 3.7 collective-permute-start.4
  50.7 3.1 collective-permute-done.4
  56.8 3.1 all-to-all-done.1
  60.8 5.1 %collective-permute-start = (f32[4,4,128]{2,1,0:T(4,128)S(1)}, f32[4,4,128]{2,1,0:T(4,128)S(1)}, u32[]{:S(2)}, u32[]{:S(2)}) collective-permute-start(f32[4,4,128]{2,1,0:T(4,128)S(1)} %get-tuple-element.208), channel_id=1, source_target_pairs={{0,8},{8,16},{16,24},{1,9},{9,17},{17,25},{2,10},{10,18},{18,26},{... | collective-permute-start | bytes 24584 | tf_op jit(solution)/shard_map/ppermute | solution.py:21
  67.5 4.0 collective-permute-done.1
  83.8 4.2 collective-permute-done.9
  90.8 4.4 collective-permute-done.10
  100.8 4.2 collective-permute-done.13
  105.2 3.1 collective-permute-start.15
  108.3 3.2 collective-permute-done.14
  117.2 4.2 collective-permute-done.17
  129.9 3.7 fusion.18
  133.6 2.9 all-to-all-start.2
  136.8 15.2 %all-to-all-done.2 = f32[32,32,128]{2,1,0:T(8,128)S(1)} async-done(((f32[32,32,128]{2,1,0:T(8,128)}), f32[32,32,128]{2,1,0:T(8,128)S(1)}, u32[]{:S(2)}, u32[]{:S(2)}) %all-to-all-start.2) | async-done | bytes 524320 | tf_op jit(solution)/shard_map/all_to_all | solution.py:182
  153.8 27.1 %while.51 = (s32[]{:T(128)}, f32[8,64,128]{2,1,0:T(8,128)S(1)}, s32[8,64,128]{2,1,0:T(8,128)S(1)}, f32[8,64,128]{2,1,0:T(8,128)}, s32[]{:T(128)}) while((s32[]{:T(128)}, f32[8,64,128]{2,1,0:T(8,128)S(1)}, s32[8,64,128]{2,1,0:T(8,128)S(1)}, f32[8,64,128]{2,1,0:T(8,128)}, s32[]{:T(128)}) %tuple.119), condition=%wide.region_12.13_spmd, body=%wide.region_10.12_spmd.sunk | while | flops 3137538 | bytes 294985 | solution.py:93
  181.7 27.3 %while.52 = (s32[]{:T(128)}, f32[8,64,128]{2,1,0:T(8,128)}, s32[8,64,128]{2,1,0:T(8,128)S(1)}, f32[8,64,128]{2,1,0:T(8,128)S(1)}, s32[]{:T(128)}) while((s32[]{:T(128)}, f32[8,64,128]{2,1,0:T(8,128)}, s32[8,64,128]{2,1,0:T(8,128)S(1)}, f32[8,64,128]{2,1,0:T(8,128)S(1)}, s32[]{:T(128)}) %tuple.125), condition=%wide.region_15.16_spmd, body=%wide.region_13.15_spmd.sunk | while | flops 3137538 | bytes 295493 | solution.py:93
  181.7 2.8 select_reduce_fusion.13
  211.0 18.4 %all_to_all.54 = f32[32,32,128]{2,1,0:T(8,128)S(1)} all-to-all(f32[32,32,128]{2,1,0:T(8,128)S(1)} %fusion.2), channel_id=1, replica_groups=mesh['lat'=4,'lon'=8] {'lat','lon'}, dimensions={0} | all-to-all | bytes 1048576 | tf_op jit(solution)/shard_map/all_to_all | solution.py:170
  230.2 3.1 collective-permute-start.20
  234.7 4.2 collective-permute-done.21
  239.1 2.8 collective-permute-start.23
  241.9 4.0 collective-permute-done.22
  251.2 4.2 collective-permute-done.25
  258.2 4.0 collective-permute-done.26
  265.3 14.0 %all-reduce = (f32[]{:T(128)}, f32[]{:T(128)}) all-reduce(f32[]{:T(128)} %get-tuple-element.118, f32[]{:T(128)} %get-tuple-element.117), channel_id=1, replica_groups=mesh['lat'=4,'lon'=8] {'lon'}, use_global_device_ids=true, to_apply=%region_8.9 | all-reduce | flops 2 | bytes 16 | tf_op jit(solution)/shard_map/psum | solution.py:10
  279.2 9.0 %all-reduce.1 = (f32[]{:T(128)}, f32[]{:T(128)}) all-reduce(f32[]{:T(128)} %get-tuple-element.159, f32[]{:T(128)} %get-tuple-element.160), channel_id=1, replica_groups=mesh['lat'=4,'lon'=8] {'lat'}, use_global_device_ids=true, to_apply=%region_9.10 | all-reduce | flops 2 | bytes 16 | tf_op jit(solution)/shard_map/psum | solution.py:9
  290.2 12.4 %psum.60 = f32[]{:T(128)} all-reduce(f32[]{:T(128)} %multiply_reduce_fusion), channel_id=1, replica_groups=mesh['lat'=4,'lon'=8] {'lon'}, use_global_device_ids=true, to_apply=%region_20.21 | all-reduce | flops 1 | bytes 8 | tf_op jit(solution)/shard_map/psum | solution.py:10
  302.7 11.0 %psum.61 = f32[]{:T(128)} all-reduce(f32[]{:T(128)} %psum.60), channel_id=1, replica_groups=mesh['lat'=4,'lon'=8] {'lat'}, use_global_device_ids=true, to_apply=%region_21.22 | all-reduce | flops 1 | bytes 8 | tf_op jit(solution)/shard_map/psum | solution.py:9
  318.2 4.2 collective-permute-done.29
  325.2 3.9 collective-permute-done.30
  334.8 4.2 collective-permute-done.33
  341.8 2.8 collective-permute-done.34
  347.0 3.7 fusion.16
  350.7 3.9 all-to-all-start.4
  354.6 15.6 %all-to-all-done.4 = f32[32,32,128]{2,1,0:T(8,128)} async-done(((f32[32,32,128]{2,1,0:T(8,128)}), f32[32,32,128]{2,1,0:T(8,128)}, u32[]{:S(2)}, u32[]{:S(2)}) %all-to-all-start.4) | async-done | bytes 524320 | tf_op jit(solution)/shard_map/all_to_all | solution.py:182
  373.0 27.1 %while.53 = (s32[]{:T(128)}, f32[8,64,128]{2,1,0:T(8,128)S(1)}, s32[8,64,128]{2,1,0:T(8,128)S(1)}, f32[8,64,128]{2,1,0:T(8,128)}, s32[]{:T(128)}) while((s32[]{:T(128)}, f32[8,64,128]{2,1,0:T(8,128)S(1)}, s32[8,64,128]{2,1,0:T(8,128)S(1)}, f32[8,64,128]{2,1,0:T(8,128)}, s32[]{:T(128)}) %tuple.121), condition=%wide.region_24.25_spmd, body=%wide.region_22.24_spmd.sunk | while | flops 3137538 | bytes 294985 | solution.py:93
  400.1 22.9 %while.54 = (s32[]{:T(128)}, f32[8,64,128]{2,1,0:T(8,128)S(1)}, s32[8,64,128]{2,1,0:T(8,128)S(1)}, f32[8,64,128]{2,1,0:T(8,128)S(1)}, s32[]{:T(128)}) while((s32[]{:T(128)}, f32[8,64,128]{2,1,0:T(8,128)S(1)}, s32[8,64,128]{2,1,0:T(8,128)S(1)}, f32[8,64,128]{2,1,0:T(8,128)S(1)}, s32[]{:T(128)}) %tuple.123), condition=%wide.region_27.28_spmd, body=%wide.region_25.27_spmd.sunk | while | flops 3137538 | bytes 294985 | solution.py:93
  400.2 2.8 select_reduce_fusion.15
  403.0 2.8 select_reduce_fusion.15
  405.9 2.8 select_reduce_fusion.15
  408.8 2.8 select_reduce_fusion.15
  411.6 2.8 select_reduce_fusion.15
  414.5 2.8 select_reduce_fusion.15
  417.3 2.8 select_reduce_fusion.15
  420.2 2.8 select_reduce_fusion.15
  424.1 18.4 %all_to_all.55 = f32[32,32,128]{2,1,0:T(8,128)S(1)} all-to-all(f32[32,32,128]{2,1,0:T(8,128)S(1)} %fusion), channel_id=1, replica_groups=mesh['lat'=4,'lon'=8] {'lat','lon'}, dimensions={0} | all-to-all | bytes 1048576 | tf_op jit(solution)/shard_map/all_to_all | solution.py:170
  443.3 3.1 collective-permute-start.36
  447.8 4.2 collective-permute-done.37
  454.8 4.3 collective-permute-done.38
  464.5 4.2 collective-permute-done.41
  471.5 3.8 collective-permute-done.42
  478.3 14.1 %psum.62 = f32[]{:T(128)} all-reduce(f32[]{:T(128)} %fusion.267), channel_id=1, replica_groups=mesh['lat'=4,'lon'=8] {'lon'}, use_global_device_ids=true, to_apply=%region_29.30 | all-reduce | flops 1 | bytes 8 | tf_op jit(solution)/shard_map/psum | solution.py:10
  492.3 9.0 %psum.63 = f32[]{:T(128)} all-reduce(f32[]{:T(128)} %psum.62), channel_id=1, replica_groups=mesh['lat'=4,'lon'=8] {'lat'}, use_global_device_ids=true, to_apply=%region_30.31 | all-reduce | flops 1 | bytes 8 | tf_op jit(solution)/shard_map/psum | solution.py:9
  (354 shorter events, 186.2 us)
Async XLA Ops:
  0.6 12.1 %copy-start.3 = (f32[512,128]{1,0:T(8,128)S(1)}, f32[512,128]{1,0:T(8,128)}, u32[]{:S(2)}) copy-start(f32[512,128]{1,0:T(8,128)} %param.26) | copy-start | bytes 786436
  3.6 10.1 %copy-start.2 = (s32[512,128]{1,0:T(8,128)S(1)}, s32[512,128]{1,0:T(8,128)}, u32[]{:S(2)}) copy-start(s32[512,128]{1,0:T(8,128)} %param.29) | copy-start | bytes 786436
  5.3 33.1 %all-to-all-start = ((s32[32,32,1]{1,2,0:T(1,128)}), s32[32,32,1]{1,2,0:T(1,128)S(1)}, u32[]{:S(2)}, u32[]{:S(2)}) async-start(s32[32,32,1]{1,2,0:T(1,128)} %sub.738), calls=%async_computation | async-start | bytes 32768 | tf_op jit(solution)/shard_map/all_to_all | solution.py:153
  38.4 5.9 %copy-start.7 = (f32[4,64,128]{2,1,0:T(8,128)S(1)}, f32[4,64,128]{2,1,0:T(8,128)}, u32[]{:S(2)}) copy-start(f32[4,64,128]{2,1,0:T(8,128)} %param.20) | copy-start | bytes 393220
  38.5 6.0 %copy-start = (f32[4,64,128]{2,1,0:T(8,128)S(1)}, f32[4,64,128]{2,1,0:T(8,128)}, u32[]{:S(2)}) copy-start(f32[4,64,128]{2,1,0:T(8,128)} %param.21) | copy-start | bytes 393220
  38.5 11.0 %copy-start.8 = (s32[64,128]{1,0:T(8,128)S(1)}, s32[64,128]{1,0:T(8,128)}, u32[]{:S(2)}) copy-start(s32[64,128]{1,0:T(8,128)} %param.23) | copy-start | bytes 98308
  38.5 21.5 %all-to-all-start.1 = ((f32[32,32,128]{2,1,0:T(8,128)}), f32[32,32,128]{2,1,0:T(8,128)S(1)}, u32[]{:S(2)}, u32[]{:S(2)}) async-start(f32[32,32,128]{2,1,0:T(8,128)} %fusion.4), calls=%async_computation.1 | async-start | bytes 1048576 | tf_op jit(solution)/shard_map/all_to_all | solution.py:170
  44.4 9.4 %collective-permute-start.4 = (f32[8,4,128]{2,1,0:T(4,128)S(1)}, f32[8,4,128]{2,1,0:T(4,128)S(1)}, u32[]{:S(2)}, u32[]{:S(2)}) collective-permute-start(f32[8,4,128]{2,1,0:T(4,128)S(1)} %get-tuple-element.168), channel_id=1, source_target_pairs={{0,8},{8,16},{16,24},{1,9},{9,17},{17,25},{2,10},{10,18},{18,26},{... | collective-permute-start | bytes 49160 | tf_op jit(solution)/shard_map/ppermute | solution.py:21
  48.1 5.8 %collective-permute-start.5 = (f32[8,4,128]{2,1,0:T(4,128)S(1)}, f32[8,4,128]{2,1,0:T(4,128)S(1)}, u32[]{:S(2)}, u32[]{:S(2)}) collective-permute-start(f32[8,4,128]{2,1,0:T(4,128)S(1)} %get-tuple-element.169), channel_id=1, source_target_pairs={{8,0},{16,8},{24,16},{9,1},{17,9},{25,17},{10,2},{18,10},{26,18},{... | collective-permute-start | bytes 49160 | tf_op jit(solution)/shard_map/ppermute | solution.py:24
  53.9 6.8 %copy-start.1 = (f32[4,64,128]{2,1,0:T(8,128)S(1)}, f32[4,64,128]{2,1,0:T(8,128)}, u32[]{:S(2)}) copy-start(f32[4,64,128]{2,1,0:T(8,128)} %param.22) | copy-start | bytes 393220
  53.9 6.8 %copy-start.9 = (f32[4]{0:T(128)S(1)}, f32[4]{0:T(128)}, u32[]{:S(2)}) copy-start(f32[4]{0:T(128)} %param.24) | copy-start | bytes 52
  54.1 13.1 %collective-permute-start.6 = (f32[8,72,4]{2,1,0:T(8,128)S(1)}, f32[8,72,4]{2,1,0:T(8,128)S(1)}, u32[]{:S(2)}, u32[]{:S(2)}) collective-permute-start(f32[8,72,4]{2,1,0:T(8,128)S(1)} %get-tuple-element.166), channel_id=1, source_target_pairs={{0,1},{1,2},{2,3},{3,4},{4,5},{5,6},{6,7},{7,0},{8,9},{9,10},{10,1... | collective-permute-start | bytes 27656 | tf_op jit(solution)/shard_map/ppermute | solution.py:21
  54.2 20.1 %collective-permute-start.7 = (f32[8,72,4]{2,1,0:T(8,128)S(1)}, f32[8,72,4]{2,1,0:T(8,128)}, u32[]{:S(2)}, u32[]{:S(2)}) collective-permute-start(f32[8,72,4]{2,1,0:T(8,128)S(1)} %get-tuple-element.167), channel_id=1, source_target_pairs={{1,0},{2,1},{3,2},{4,3},{5,4},{6,5},{7,6},{0,7},{9,8},{10,9},{11,1... | collective-permute-start | bytes 27656 | tf_op jit(solution)/shard_map/ppermute | solution.py:24
  60.8 6.7 %collective-permute-start = (f32[4,4,128]{2,1,0:T(4,128)S(1)}, f32[4,4,128]{2,1,0:T(4,128)S(1)}, u32[]{:S(2)}, u32[]{:S(2)}) collective-permute-start(f32[4,4,128]{2,1,0:T(4,128)S(1)} %get-tuple-element.208), channel_id=1, source_target_pairs={{0,8},{8,16},{16,24},{1,9},{9,17},{17,25},{2,10},{10,18},{18,26},{... | collective-permute-start | bytes 24584 | tf_op jit(solution)/shard_map/ppermute | solution.py:21
  65.9 5.5 %collective-permute-start.1 = (f32[4,4,128]{2,1,0:T(4,128)S(1)}, f32[4,4,128]{2,1,0:T(4,128)S(1)}, u32[]{:S(2)}, u32[]{:S(2)}) collective-permute-start(f32[4,4,128]{2,1,0:T(4,128)S(1)} %get-tuple-element.209), channel_id=1, source_target_pairs={{8,0},{16,8},{24,16},{9,1},{17,9},{25,17},{10,2},{18,10},{26,18},{... | collective-permute-start | bytes 24584 | tf_op jit(solution)/shard_map/ppermute | solution.py:24
  71.6 6.2 %collective-permute-start.2 = (f32[4,72,4]{2,1,0:T(8,128)S(1)}, f32[4,72,4]{2,1,0:T(8,128)S(1)}, u32[]{:S(2)}, u32[]{:S(2)}) collective-permute-start(f32[4,72,4]{2,1,0:T(8,128)S(1)} %get-tuple-element.188), channel_id=1, source_target_pairs={{0,1},{1,2},{2,3},{3,4},{4,5},{5,6},{6,7},{7,0},{8,9},{9,10},{10,1... | collective-permute-start | bytes 13832 | tf_op jit(solution)/shard_map/ppermute | solution.py:21
  71.6 6.1 %collective-permute-start.3 = (f32[4,72,4]{2,1,0:T(8,128)S(1)}, f32[4,72,4]{2,1,0:T(8,128)S(1)}, u32[]{:S(2)}, u32[]{:S(2)}) collective-permute-start(f32[4,72,4]{2,1,0:T(8,128)S(1)} %get-tuple-element.189), channel_id=1, source_target_pairs={{1,0},{2,1},{3,2},{4,3},{5,4},{6,5},{7,6},{0,7},{9,8},{10,9},{11,1... | collective-permute-start | bytes 13832 | tf_op jit(solution)/shard_map/ppermute | solution.py:24
  80.2 3.5 collective-permute-start.8
  82.4 5.5 %collective-permute-start.9 = (f32[4,4,128]{2,1,0:T(4,128)S(1)}, f32[4,4,128]{2,1,0:T(4,128)S(1)}, u32[]{:S(2)}, u32[]{:S(2)}) collective-permute-start(f32[4,4,128]{2,1,0:T(4,128)S(1)} %get-tuple-element.207), channel_id=1, source_target_pairs={{8,0},{16,8},{24,16},{9,1},{17,9},{25,17},{10,2},{18,10},{26,18},{... | collective-permute-start | bytes 24584 | tf_op jit(solution)/shard_map/ppermute | solution.py:24
  88.1 7.1 %collective-permute-start.10 = (f32[4,72,4]{2,1,0:T(8,128)S(1)}, f32[4,72,4]{2,1,0:T(8,128)S(1)}, u32[]{:S(2)}, u32[]{:S(2)}) collective-permute-start(f32[4,72,4]{2,1,0:T(8,128)S(1)} %get-tuple-element.186), channel_id=1, source_target_pairs={{0,1},{1,2},{2,3},{3,4},{4,5},{5,6},{6,7},{7,0},{8,9},{9,10},{10,1... | collective-permute-start | bytes 13832 | tf_op jit(solution)/shard_map/ppermute | solution.py:21
  88.1 7.0 %collective-permute-start.11 = (f32[4,72,4]{2,1,0:T(8,128)S(1)}, f32[4,72,4]{2,1,0:T(8,128)S(1)}, u32[]{:S(2)}, u32[]{:S(2)}) collective-permute-start(f32[4,72,4]{2,1,0:T(8,128)S(1)} %get-tuple-element.187), channel_id=1, source_target_pairs={{1,0},{2,1},{3,2},{4,3},{5,4},{6,5},{7,6},{0,7},{9,8},{10,9},{11,1... | collective-permute-start | bytes 13832 | tf_op jit(solution)/shard_map/ppermute | solution.py:24
  97.6 3.3 collective-permute-start.12
  99.5 5.5 %collective-permute-start.13 = (f32[4,4,128]{2,1,0:T(4,128)S(1)}, f32[4,4,128]{2,1,0:T(4,128)S(1)}, u32[]{:S(2)}, u32[]{:S(2)}) collective-permute-start(f32[4,4,128]{2,1,0:T(4,128)S(1)} %get-tuple-element.205), channel_id=1, source_target_pairs={{8,0},{16,8},{24,16},{9,1},{17,9},{25,17},{10,2},{18,10},{26,18},{... | collective-permute-start | bytes 24584 | tf_op jit(solution)/shard_map/ppermute | solution.py:24
  105.2 6.4 %collective-permute-start.14 = (f32[4,72,4]{2,1,0:T(8,128)S(1)}, f32[4,72,4]{2,1,0:T(8,128)S(1)}, u32[]{:S(2)}, u32[]{:S(2)}) collective-permute-start(f32[4,72,4]{2,1,0:T(8,128)S(1)} %get-tuple-element.184), channel_id=1, source_target_pairs={{0,1},{1,2},{2,3},{3,4},{4,5},{5,6},{6,7},{7,0},{8,9},{9,10},{10,1... | collective-permute-start | bytes 13832 | tf_op jit(solution)/shard_map/ppermute | solution.py:21
  105.2 6.3 %collective-permute-start.15 = (f32[4,72,4]{2,1,0:T(8,128)S(1)}, f32[4,72,4]{2,1,0:T(8,128)S(1)}, u32[]{:S(2)}, u32[]{:S(2)}) collective-permute-start(f32[4,72,4]{2,1,0:T(8,128)S(1)} %get-tuple-element.185), channel_id=1, source_target_pairs={{1,0},{2,1},{3,2},{4,3},{5,4},{6,5},{7,6},{0,7},{9,8},{10,9},{11,1... | collective-permute-start | bytes 13832 | tf_op jit(solution)/shard_map/ppermute | solution.py:24
  114.0 3.3 collective-permute-start.16
  115.9 5.5 %collective-permute-start.17 = (f32[4,4,128]{2,1,0:T(4,128)S(1)}, f32[4,4,128]{2,1,0:T(4,128)S(1)}, u32[]{:S(2)}, u32[]{:S(2)}) collective-permute-start(f32[4,4,128]{2,1,0:T(4,128)S(1)} %get-tuple-element.203), channel_id=1, source_target_pairs={{8,0},{16,8},{24,16},{9,1},{17,9},{25,17},{10,2},{18,10},{26,18},{... | collective-permute-start | bytes 24584 | tf_op jit(solution)/shard_map/ppermute | solution.py:24
  121.6 5.9 %collective-permute-start.18 = (f32[4,72,4]{2,1,0:T(8,128)S(1)}, f32[4,72,4]{2,1,0:T(8,128)S(1)}, u32[]{:S(2)}, u32[]{:S(2)}) collective-permute-start(f32[4,72,4]{2,1,0:T(8,128)S(1)} %get-tuple-element.182), channel_id=1, source_target_pairs={{0,1},{1,2},{2,3},{3,4},{4,5},{5,6},{6,7},{7,0},{8,9},{9,10},{10,1... | collective-permute-start | bytes 13832 | tf_op jit(solution)/shard_map/ppermute | solution.py:21
  121.6 5.9 %collective-permute-start.19 = (f32[4,72,4]{2,1,0:T(8,128)S(1)}, f32[4,72,4]{2,1,0:T(8,128)S(1)}, u32[]{:S(2)}, u32[]{:S(2)}) collective-permute-start(f32[4,72,4]{2,1,0:T(8,128)S(1)} %get-tuple-element.183), channel_id=1, source_target_pairs={{1,0},{2,1},{3,2},{4,3},{5,4},{6,5},{7,6},{0,7},{9,8},{10,9},{11,1... | collective-permute-start | bytes 13832 | tf_op jit(solution)/shard_map/ppermute | solution.py:24
  129.9 3.7 copy-start.5
  133.6 18.5 %all-to-all-start.2 = ((f32[32,32,128]{2,1,0:T(8,128)}), f32[32,32,128]{2,1,0:T(8,128)S(1)}, u32[]{:S(2)}, u32[]{:S(2)}) async-start(f32[32,32,128]{2,1,0:T(8,128)} %fusion.18), calls=%async_computation.2 | async-start | bytes 1048576 | tf_op jit(solution)/shard_map/all_to_all | solution.py:182
  230.2 4.5 collective-permute-start.20
  233.4 5.5 %collective-permute-start.21 = (f32[4,4,128]{2,1,0:T(4,128)S(1)}, f32[4,4,128]{2,1,0:T(4,128)S(1)}, u32[]{:S(2)}, u32[]{:S(2)}) collective-permute-start(f32[4,4,128]{2,1,0:T(4,128)S(1)} %get-tuple-element.201), channel_id=1, source_target_pairs={{8,0},{16,8},{24,16},{9,1},{17,9},{25,17},{10,2},{18,10},{26,18},{... | collective-permute-start | bytes 24584 | tf_op jit(solution)/shard_map/ppermute | solution.py:24
  239.0 6.8 %collective-permute-start.22 = (f32[4,72,4]{2,1,0:T(8,128)S(1)}, f32[4,72,4]{2,1,0:T(8,128)S(1)}, u32[]{:S(2)}, u32[]{:S(2)}) collective-permute-start(f32[4,72,4]{2,1,0:T(8,128)S(1)} %get-tuple-element.180), channel_id=1, source_target_pairs={{0,1},{1,2},{2,3},{3,4},{4,5},{5,6},{6,7},{7,0},{8,9},{9,10},{10,1... | collective-permute-start | bytes 13832 | tf_op jit(solution)/shard_map/ppermute | solution.py:21
  239.1 6.8 %collective-permute-start.23 = (f32[4,72,4]{2,1,0:T(8,128)S(1)}, f32[4,72,4]{2,1,0:T(8,128)S(1)}, u32[]{:S(2)}, u32[]{:S(2)}) collective-permute-start(f32[4,72,4]{2,1,0:T(8,128)S(1)} %get-tuple-element.181), channel_id=1, source_target_pairs={{1,0},{2,1},{3,2},{4,3},{5,4},{6,5},{7,6},{0,7},{9,8},{10,9},{11,1... | collective-permute-start | bytes 13832 | tf_op jit(solution)/shard_map/ppermute | solution.py:24
  248.3 2.9 collective-permute-start.24
  249.9 5.5 %collective-permute-start.25 = (f32[4,4,128]{2,1,0:T(4,128)S(1)}, f32[4,4,128]{2,1,0:T(4,128)S(1)}, u32[]{:S(2)}, u32[]{:S(2)}) collective-permute-start(f32[4,4,128]{2,1,0:T(4,128)S(1)} %get-tuple-element.199), channel_id=1, source_target_pairs={{8,0},{16,8},{24,16},{9,1},{17,9},{25,17},{10,2},{18,10},{26,18},{... | collective-permute-start | bytes 24584 | tf_op jit(solution)/shard_map/ppermute | solution.py:24
  255.5 6.7 %collective-permute-start.26 = (f32[4,72,4]{2,1,0:T(8,128)S(1)}, f32[4,72,4]{2,1,0:T(8,128)S(1)}, u32[]{:S(2)}, u32[]{:S(2)}) collective-permute-start(f32[4,72,4]{2,1,0:T(8,128)S(1)} %get-tuple-element.178), channel_id=1, source_target_pairs={{0,1},{1,2},{2,3},{3,4},{4,5},{5,6},{6,7},{7,0},{8,9},{9,10},{10,1... | collective-permute-start | bytes 13832 | tf_op jit(solution)/shard_map/ppermute | solution.py:21
  255.6 6.6 %collective-permute-start.27 = (f32[4,72,4]{2,1,0:T(8,128)S(1)}, f32[4,72,4]{2,1,0:T(8,128)S(1)}, u32[]{:S(2)}, u32[]{:S(2)}) collective-permute-start(f32[4,72,4]{2,1,0:T(8,128)S(1)} %get-tuple-element.179), channel_id=1, source_target_pairs={{1,0},{2,1},{3,2},{4,3},{5,4},{6,5},{7,6},{0,7},{9,8},{10,9},{11,1... | collective-permute-start | bytes 13832 | tf_op jit(solution)/shard_map/ppermute | solution.py:24
  315.0 3.2 collective-permute-start.28
  316.9 5.5 %collective-permute-start.29 = (f32[4,4,128]{2,1,0:T(4,128)S(1)}, f32[4,4,128]{2,1,0:T(4,128)S(1)}, u32[]{:S(2)}, u32[]{:S(2)}) collective-permute-start(f32[4,4,128]{2,1,0:T(4,128)S(1)} %get-tuple-element.197), channel_id=1, source_target_pairs={{8,0},{16,8},{24,16},{9,1},{17,9},{25,17},{10,2},{18,10},{26,18},{... | collective-permute-start | bytes 24584 | tf_op jit(solution)/shard_map/ppermute | solution.py:24
  322.5 6.6 %collective-permute-start.30 = (f32[4,72,4]{2,1,0:T(8,128)S(1)}, f32[4,72,4]{2,1,0:T(8,128)S(1)}, u32[]{:S(2)}, u32[]{:S(2)}) collective-permute-start(f32[4,72,4]{2,1,0:T(8,128)S(1)} %get-tuple-element.176), channel_id=1, source_target_pairs={{0,1},{1,2},{2,3},{3,4},{4,5},{5,6},{6,7},{7,0},{8,9},{9,10},{10,1... | collective-permute-start | bytes 13832 | tf_op jit(solution)/shard_map/ppermute | solution.py:21
  322.6 6.5 %collective-permute-start.31 = (f32[4,72,4]{2,1,0:T(8,128)S(1)}, f32[4,72,4]{2,1,0:T(8,128)S(1)}, u32[]{:S(2)}, u32[]{:S(2)}) collective-permute-start(f32[4,72,4]{2,1,0:T(8,128)S(1)} %get-tuple-element.177), channel_id=1, source_target_pairs={{1,0},{2,1},{3,2},{4,3},{5,4},{6,5},{7,6},{0,7},{9,8},{10,9},{11,1... | collective-permute-start | bytes 13832 | tf_op jit(solution)/shard_map/ppermute | solution.py:24
  331.5 3.3 collective-permute-start.32
  333.4 5.5 %collective-permute-start.33 = (f32[4,4,128]{2,1,0:T(4,128)S(1)}, f32[4,4,128]{2,1,0:T(4,128)S(1)}, u32[]{:S(2)}, u32[]{:S(2)}) collective-permute-start(f32[4,4,128]{2,1,0:T(4,128)S(1)} %get-tuple-element.195), channel_id=1, source_target_pairs={{8,0},{16,8},{24,16},{9,1},{17,9},{25,17},{10,2},{18,10},{26,18},{... | collective-permute-start | bytes 24584 | tf_op jit(solution)/shard_map/ppermute | solution.py:24
  339.1 5.5 %collective-permute-start.34 = (f32[4,72,4]{2,1,0:T(8,128)S(1)}, f32[4,72,4]{2,1,0:T(8,128)S(1)}, u32[]{:S(2)}, u32[]{:S(2)}) collective-permute-start(f32[4,72,4]{2,1,0:T(8,128)S(1)} %get-tuple-element.174), channel_id=1, source_target_pairs={{0,1},{1,2},{2,3},{3,4},{4,5},{5,6},{6,7},{7,0},{8,9},{9,10},{10,1... | collective-permute-start | bytes 13832 | tf_op jit(solution)/shard_map/ppermute | solution.py:21
  339.2 5.5 %collective-permute-start.35 = (f32[4,72,4]{2,1,0:T(8,128)S(1)}, f32[4,72,4]{2,1,0:T(8,128)S(1)}, u32[]{:S(2)}, u32[]{:S(2)}) collective-permute-start(f32[4,72,4]{2,1,0:T(8,128)S(1)} %get-tuple-element.175), channel_id=1, source_target_pairs={{1,0},{2,1},{3,2},{4,3},{5,4},{6,5},{7,6},{0,7},{9,8},{10,9},{11,1... | collective-permute-start | bytes 13832 | tf_op jit(solution)/shard_map/ppermute | solution.py:24
  350.7 19.5 %all-to-all-start.4 = ((f32[32,32,128]{2,1,0:T(8,128)}), f32[32,32,128]{2,1,0:T(8,128)}, u32[]{:S(2)}, u32[]{:S(2)}) async-start(f32[32,32,128]{2,1,0:T(8,128)} %fusion.16), calls=%async_computation.4 | async-start | bytes 1048576 | tf_op jit(solution)/shard_map/all_to_all | solution.py:182
  443.3 4.5 collective-permute-start.36
  446.5 5.5 %collective-permute-start.37 = (f32[4,4,128]{2,1,0:T(4,128)S(1)}, f32[4,4,128]{2,1,0:T(4,128)S(1)}, u32[]{:S(2)}, u32[]{:S(2)}) collective-permute-start(f32[4,4,128]{2,1,0:T(4,128)S(1)} %get-tuple-element.193), channel_id=1, source_target_pairs={{8,0},{16,8},{24,16},{9,1},{17,9},{25,17},{10,2},{18,10},{26,18},{... | collective-permute-start | bytes 24584 | tf_op jit(solution)/shard_map/ppermute | solution.py:24
  452.1 7.0 %collective-permute-start.38 = (f32[4,72,4]{2,1,0:T(8,128)S(1)}, f32[4,72,4]{2,1,0:T(8,128)S(1)}, u32[]{:S(2)}, u32[]{:S(2)}) collective-permute-start(f32[4,72,4]{2,1,0:T(8,128)S(1)} %get-tuple-element.172), channel_id=1, source_target_pairs={{0,1},{1,2},{2,3},{3,4},{4,5},{5,6},{6,7},{7,0},{8,9},{9,10},{10,1... | collective-permute-start | bytes 13832 | tf_op jit(solution)/shard_map/ppermute | solution.py:21
  452.2 6.9 %collective-permute-start.39 = (f32[4,72,4]{2,1,0:T(8,128)S(1)}, f32[4,72,4]{2,1,0:T(8,128)S(1)}, u32[]{:S(2)}, u32[]{:S(2)}) collective-permute-start(f32[4,72,4]{2,1,0:T(8,128)S(1)} %get-tuple-element.173), channel_id=1, source_target_pairs={{1,0},{2,1},{3,2},{4,3},{5,4},{6,5},{7,6},{0,7},{9,8},{10,9},{11,1... | collective-permute-start | bytes 13832 | tf_op jit(solution)/shard_map/ppermute | solution.py:24
  461.5 2.9 collective-permute-start.40
  463.1 5.5 %collective-permute-start.41 = (f32[4,4,128]{2,1,0:T(4,128)S(1)}, f32[4,4,128]{2,1,0:T(4,128)S(1)}, u32[]{:S(2)}, u32[]{:S(2)}) collective-permute-start(f32[4,4,128]{2,1,0:T(4,128)S(1)} %get-tuple-element.191), channel_id=1, source_target_pairs={{8,0},{16,8},{24,16},{9,1},{17,9},{25,17},{10,2},{18,10},{26,18},{... | collective-permute-start | bytes 24584 | tf_op jit(solution)/shard_map/ppermute | solution.py:24
  468.8 6.5 %collective-permute-start.42 = (f32[4,72,4]{2,1,0:T(8,128)S(1)}, f32[4,72,4]{2,1,0:T(8,128)S(1)}, u32[]{:S(2)}, u32[]{:S(2)}) collective-permute-start(f32[4,72,4]{2,1,0:T(8,128)S(1)} %get-tuple-element.170), channel_id=1, source_target_pairs={{0,1},{1,2},{2,3},{3,4},{4,5},{5,6},{6,7},{7,0},{8,9},{9,10},{10,1... | collective-permute-start | bytes 13832 | tf_op jit(solution)/shard_map/ppermute | solution.py:21
  468.8 6.4 %collective-permute-start.43 = (f32[4,72,4]{2,1,0:T(8,128)S(1)}, f32[4,72,4]{2,1,0:T(8,128)S(1)}, u32[]{:S(2)}, u32[]{:S(2)}) collective-permute-start(f32[4,72,4]{2,1,0:T(8,128)S(1)} %get-tuple-element.171), channel_id=1, source_target_pairs={{1,0},{2,1},{3,2},{4,3},{5,4},{6,5},{7,6},{0,7},{9,8},{10,9},{11,1... | collective-permute-start | bytes 13832 | tf_op jit(solution)/shard_map/ppermute | solution.py:24
  477.5 25.2 %copy-start.4 = (f32[512,128]{1,0:T(8,128)S(1)}, f32[512,128]{1,0:T(8,128)}, u32[]{:S(2)}) copy-start(f32[512,128]{1,0:T(8,128)} %param.25) | copy-start | bytes 786436
  478.3 25.1 %copy-start.6 = (f32[4,64,128]{2,1,0:T(8,128)S(1)}, f32[4,64,128]{2,1,0:T(8,128)}, u32[]{:S(2)}) copy-start(f32[4,64,128]{2,1,0:T(8,128)} %copy-done.5) | copy-start | bytes 393220
